TPU v7x, 32 devices: a whole 2x2x4 slice. The times are simulated.
32 devices in a mesh: rows: 8 (over z, x), cols: 4 (over y, core).
Axes of the slice: x: 2, y: 2, z: 4, core: 2. Of those that a mesh axis runs over, the one named last changes fastest.
Arguments:
- panel_t: float32 [16, 2048], P(None, ('rows', 'cols')), may hold values from -6 to 6
- kinship: float32 [2048, 2048], P('rows', 'cols'), may hold values from -0.125 to 0.125
Outputs:
- kin_panel_t: float32 [16, 2048], P(None, ('rows', 'cols'))
- score: float32 [16, 16], replicated
All inputs are finite; a program needn't handle non-finite values.
Results may differ from a plain program's by a relative error of at most 0.00008.
Values sent between devices are 32-bit elements; how exact they have to be, the bound alone decides.
A program may use at most 64 MiB of HBM per device.

v0:
```python
import jax
import jax.numpy as jnp
from jax import lax
from jax.sharding import PartitionSpec as P


def contract(left, right):
    return lax.dot_general(
        left,
        right,
        (((1,), (1,)), ((), ())),
        precision=lax.Precision.HIGHEST,
        preferred_element_type=jnp.float32,
    )


def shards(panel_t, kinship):
    slab_rows, block_cols = kinship.shape
    row_index = lax.axis_index("rows")
    col_index = lax.axis_index("cols")
    gathered = lax.all_gather(panel_t, ("rows", "cols"), axis=1, tiled=True)
    slab_panel = lax.dynamic_slice_in_dim(gathered, row_index * slab_rows, slab_rows, 1)
    block_panel = lax.dynamic_slice_in_dim(gathered, col_index * block_cols, block_cols, 1)
    partial_value = contract(block_panel, kinship)
    scale = jnp.sqrt(jnp.float32(gathered.shape[1]))
    early_sum = lax.psum(contract(slab_panel, partial_value), ("rows", "cols"))
    kin_panel_t = lax.psum_scatter(partial_value, "cols", scatter_dimension=1, tiled=True)
    return (kin_panel_t, early_sum / scale)


def solution(mesh):
    placed = (P(None, ("rows", "cols")), P("rows", "cols"))
    return jax.shard_map(
        shards,
        mesh=mesh,
        in_specs=placed,
        out_specs=(P(None, ("rows", "cols")), P()),
        check_vma=False,
    )
```

profile of v0, /device:TPU:0, one launch (start us, length us, event | category | flops | bytes accessed | tf_op | source)
XLA Modules:
  0.0 99.0 jit_solution(12220211806638438616)
XLA Ops:
  7.2 0.0 copy-start
  7.2 0.0 reduce-scatter.4.cloned.1.call-start
  7.2 44.3 %all-gather = f32[32,64,16]{1,2,0:T(8,128)S(1)} all-gather(f32[1,64,16]{1,2,0:T(8,128)} %bitcast.11), channel_id=1, replica_groups=mesh['rows'=8,'cols'=4] {'rows','cols'}, dimensions={0}, use_global_device_ids=true | all-gather | bytes 135168 | tf_op jit(solution)/shard_map/all_gather | solution.py:21
  51.6 0.1 copy.5
  51.7 0.1 reshape.5
  51.8 0.0 copy-done
  51.8 0.5 fusion
  52.3 0.8 copy.6
  53.1 0.0 reduce-scatter.4.cloned.1.call-update
  53.1 0.1 fusion.2
  53.2 36.9 %psum.7 = f32[16,16]{1,0:T(8,128)S(1)} all-reduce(f32[16,16]{1,0:T(8,128)S(1)} %fusion.2), channel_id=1, replica_groups=mesh['rows'=8,'cols'=4] {'rows','cols'}, use_global_device_ids=true, to_apply=%region_1.0 | all-reduce | flops 256 | bytes 2048 | tf_op jit(solution)/shard_map/psum | solution.py:26
  90.1 0.6 broadcast_multiply_fusion
  90.7 0.0 reduce-scatter.4.cloned.1.call-done
  90.7 1.4 %copy.7 = f32[16,64]{1,0:T(8,128)} copy(f32[16,64]{0,1:T(8,128)} %bitcast.10) | data formatting | bytes 8192
Async XLA Ops:
  7.2 44.6 %copy-start = (f32[256,512]{1,0:T(8,128)S(1)}, f32[256,512]{1,0:T(8,128)}, u32[]{:S(2)}) copy-start(f32[256,512]{1,0:T(8,128)} %param.3) | copy-start | bytes 1572868
  7.2 83.5 %reduce-scatter.4.cloned.1.call-start = ((), (), s32[]{:S(2)}) async-start(), calls=%async_computation.1 | async-start | bytes 163840
Sparse Core Ops, SparseCore 0:
  53.2 15.7 reduce-scatter.3
where the time goes:
time: 99.9 us; the launch traced here: 99 us
  blocking collectives  81.2 us (81%)
  between operations  14.1 us (14%)
  local copies, waits for them, and re-layouts  2.39 us (2%)
    all_gather x1, blocking collectives, shards(): gathered = lax.all_gather(panel_t, ('rows', 'cols'), axis=1, tiled=True)  44.3 us
    psum x1, blocking collectives, shards(): early_sum = lax.psum(contract(slab_panel, partial_value), ('rows', 'cols'))  36.9 us
    unnamed x5, local copies, waits for them, and re-layouts  2.31 us
  transfers between devices with their start and end apart: 1, of which 0 were waited for; matrix products, arithmetic and copies ran while one was open for 1% of the time, Pallas kernels for 0%

commit v1 on v0

v1 whole, which is shorter than its diff:
```python
import functools
import math

import jax
import jax.numpy as jnp
from jax import lax
from jax.experimental import pallas as pl
from jax.experimental.pallas import tpu as pltpu
from jax.sharding import PartitionSpec as P

MESH = pl.DeviceIdType.MESH
LANES = 128
SUBLANES = 8


def dot(left, right, contract):
    return lax.dot_general(
        left,
        right,
        (contract, ((), ())),
        precision=lax.Precision.HIGHEST,
        preferred_element_type=jnp.float32,
    )


def group_mask(traits):
    row = lax.broadcasted_iota(jnp.int32, (traits, LANES), 0)
    lane = lax.broadcasted_iota(jnp.int32, (traits, LANES), 1)
    return (row % SUBLANES) == (lane // traits)


def kernel(
    rows,
    cols,
    panel_hbm,
    kin_hbm,
    out_ref,
    score_ref,
    panel,
    kin,
    zbuf,
    slab,
    block,
    part,
    landed,
    form,
    plane_forms,
    line_form,
    line_forms,
    local_sem,
    z_send,
    z_recv,
    slab_send,
    slab_recv,
    block_send,
    block_recv,
    part_send,
    part_recv,
    plane_send,
    plane_recv,
    line_send,
    line_recv,
):
    depth = rows // cols
    plane = depth * cols
    traits, own = panel.shape
    row, col = lax.axis_index("rows"), lax.axis_index("cols")
    zz, xx = row // depth, row % depth
    mine = xx * cols + col

    def z_mate(k):
        return (k * depth + xx, col)

    def plane_mate(m):
        return (zz * depth + m // cols, m % cols)

    get_panel = pltpu.make_async_copy(panel_hbm, panel, local_sem.at[0])
    get_panel.start()
    get_kin = pltpu.make_async_copy(kin_hbm, kin, local_sem.at[1])
    get_kin.start()

    barrier = pltpu.get_barrier_semaphore()
    for step in range(1, cols):
        pl.semaphore_signal(
            barrier, inc=1, device_id=z_mate((zz + step) % cols), device_id_type=MESH
        )
    for step in range(1, plane):
        pl.semaphore_signal(
            barrier, inc=1, device_id=plane_mate((mine + step) % plane), device_id_type=MESH
        )
    get_panel.wait()
    keep_line = pltpu.make_async_copy(panel, zbuf.at[zz], z_recv.at[zz])
    keep_line.start()
    keep_slab = pltpu.make_async_copy(panel, slab.at[col], slab_recv.at[col])
    keep_slab.start()
    pl.semaphore_wait(barrier, cols - 1 + plane - 1)

    def remote(src, dst, send, recv, where):
        return pltpu.make_async_remote_copy(
            src_ref=src,
            dst_ref=dst,
            send_sem=send,
            recv_sem=recv,
            device_id=where,
            device_id_type=MESH,
        )

    sends = []
    for step in range(1, cols):
        k = (zz + step) % cols
        copy = remote(panel, zbuf.at[zz], z_send.at[step], z_recv.at[zz], z_mate(k))
        copy.start()
        sends.append(copy)
    for step in range(1, cols):
        c = (col + step) % cols
        copy = remote(panel, slab.at[col], slab_send.at[step], slab_recv.at[col], (row, c))
        copy.start()
        sends.append(copy)

    def arrived(buf, sem, slot):
        remote(buf.at[slot], buf.at[slot], sem.at[slot], sem.at[slot], (row, col)).wait_recv()

    keep_slab.wait()
    for step in range(1, cols):
        arrived(slab, slab_recv, (col + step) % cols)
    get_kin.wait()
    slab_panel = jnp.concatenate([slab[c] for c in range(cols)], axis=1)
    side = dot(slab_panel, kin[...], ((1,), (0,)))

    keep_line.wait()
    for step in range(1, cols):
        arrived(zbuf, z_recv, (zz + step) % cols)
    keep_block = pltpu.make_async_copy(zbuf.at[col], block.at[mine], block_recv.at[mine])
    keep_block.start()
    for step in range(1, plane):
        m = (mine + step) % plane
        copy = remote(
            zbuf.at[m % cols], block.at[mine], block_send.at[step], block_recv.at[mine], plane_mate(m)
        )
        copy.start()
        sends.append(copy)
    keep_block.wait()
    for step in range(1, plane):
        arrived(block, block_recv, (mine + step) % plane)

    block_panel = jnp.concatenate([block[m] for m in range(plane)], axis=1)
    wide = jnp.concatenate([block_panel] * (LANES // traits), axis=0)
    spread = dot(side, wide, ((1,), (1,)))
    mask = group_mask(traits)
    spread = jnp.where(mask, spread, 0.0)
    form[...] = jnp.sum(spread.reshape(traits // SUBLANES, SUBLANES, LANES), axis=1)
    for step in range(1, plane):
        m = (mine + step) % plane
        copy = remote(
            form, plane_forms.at[mine], plane_send.at[step], plane_recv.at[mine], plane_mate(m)
        )
        copy.start()
        sends.append(copy)
    plane_forms[mine] = form[...]

    value = dot(block_panel, kin[...], ((1,), (1,)))
    for c in range(cols):
        part[c] = value[:, c * own : (c + 1) * own]
    for step in range(1, cols):
        c = (col + step) % cols
        copy = remote(part.at[c], landed.at[col], part_send.at[step], part_recv.at[col], (row, c))
        copy.start()
        sends.append(copy)
    landed[col] = part[col]

    for step in range(1, plane):
        arrived(plane_forms, plane_recv, (mine + step) % plane)
    total = plane_forms[0]
    for m in range(1, plane):
        total += plane_forms[m]
    line_form[...] = total
    for step in range(1, cols):
        k = (zz + step) % cols
        copy = remote(
            line_form, line_forms.at[zz], line_send.at[step], line_recv.at[zz], z_mate(k)
        )
        copy.start()
        sends.append(copy)
    line_forms[zz] = total

    for step in range(1, cols):
        arrived(landed, part_recv, (col + step) % cols)
    result = landed[0]
    for c in range(1, cols):
        result += landed[c]
    out_ref[...] = result

    for step in range(1, cols):
        arrived(line_forms, line_recv, (zz + step) % cols)
    total = line_forms[0]
    for k in range(1, cols):
        total += line_forms[k]
    spread = jnp.concatenate(
        [
            jnp.broadcast_to(total[i : i + 1, :], (SUBLANES, LANES))
            for i in range(traits // SUBLANES)
        ],
        axis=0,
    )
    spread = jnp.where(mask, spread, 0.0)
    shift = LANES // 2
    while shift >= traits:
        spread += pltpu.roll(spread, shift, 1)
        shift //= 2
    score_ref[...] = spread[:, :traits] / math.sqrt(rows * cols * own)
    for copy in sends:
        copy.wait_send()


def shards(rows, cols, panel_t, kinship):
    traits, own = panel_t.shape
    plane = rows // cols * cols
    vmem = pltpu.VMEM
    dma = pltpu.SemaphoreType.DMA
    form = (traits * traits // LANES, LANES)
    f32 = jnp.float32
    return tuple(
        pl.pallas_call(
            functools.partial(kernel, rows, cols),
            out_shape=(
                jax.ShapeDtypeStruct((traits, own), f32),
                jax.ShapeDtypeStruct((traits, traits), f32),
            ),
            in_specs=[pl.BlockSpec(memory_space=pl.ANY)] * 2,
            out_specs=(pl.BlockSpec(memory_space=vmem),) * 2,
            scratch_shapes=[
                vmem((traits, own), f32),
                vmem(kinship.shape, f32),
                vmem((cols, traits, own), f32),
                vmem((cols, traits, own), f32),
                vmem((plane, traits, own), f32),
                vmem((cols, traits, own), f32),
                vmem((cols, traits, own), f32),
                vmem(form, f32),
                vmem((plane,) + form, f32),
                vmem(form, f32),
                vmem((cols,) + form, f32),
                dma((2,)),
                dma((cols,)),
                dma((cols,)),
                dma((cols,)),
                dma((cols,)),
                dma((plane,)),
                dma((plane,)),
                dma((cols,)),
                dma((cols,)),
                dma((plane,)),
                dma((plane,)),
                dma((cols,)),
                dma((cols,)),
            ],
            compiler_params=pltpu.CompilerParams(collective_id=0, has_side_effects=True),
        )(panel_t, kinship)
    )


def solution(mesh):
    rows, cols = mesh.shape["rows"], mesh.shape["cols"]
    return jax.shard_map(
        functools.partial(shards, rows, cols),
        mesh=mesh,
        in_specs=(P(None, ("rows", "cols")), P("rows", "cols")),
        out_specs=(P(None, ("rows", "cols")), P()),
        check_vma=False,
    )
```

time: 99.9 us -> 23.5 us (0.24)
  blocking collectives: 81.2 us -> 0 us
  Pallas kernels: 0 us -> 20.7 us
  between operations: 14.1 us -> 0.65 us
    all_gather x1 -> x0, blocking collectives: 44.3 us -> none  [shards(): gathered = lax.all_gather(panel_t, ('rows', 'cols'), axis=1, tiled=True)]
    psum x1 -> x0, blocking collectives: 36.9 us -> none  [shards(): early_sum = lax.psum(contract(slab_panel, partial_value), ('rows', 'cols'))]
    pallas_call x0 -> x1, Pallas kernels: none -> 20.7 us  [shards(): pl.pallas_call(functools.partial(kernel, rows, cols), out_shape=(jax.Shap...]
    unnamed x5 -> x4, local copies, waits for them, and re-layouts: 2.31 us -> 1.9 us
  transfers between devices with their start and end apart: 1 -> 0, of which waited for: 0 -> 0; matrix products, arithmetic and copies ran while one was open for 1% -> 0% of each run, Pallas kernels for 0% -> 0%
where the time goes in v1:
time: 23.5 us; the launch traced here: 23.3 us
  Pallas kernels  20.7 us (88%)
  local copies, waits for them, and re-layouts  1.9 us (8%)
  between operations  0.65 us (3%)
    pallas_call x1, Pallas kernels, shards(): pl.pallas_call(functools.partial(kernel, rows, cols), out_shape=(jax.Shap...  20.7 us
    unnamed x4, local copies, waits for them, and re-layouts  1.9 us

profile of v1, /device:TPU:0, one launch (start us, length us, event | category | flops | bytes accessed | tf_op | source)
XLA Modules:
  0.0 23.3 jit_solution(15279760277349172605)
XLA Ops:
  0.6 20.7 %shard_map.41 = (f32[16,64]{1,0:T(8,128)}, f32[16,16]{1,0:T(8,128)}) custom-call(f32[16,64]{1,0:T(8,128)} %panel_hbm.1, f32[256,512]{1,0:T(8,128)} %kin_hbm.1), custom_call_target="tpu_custom_call" | custom-call | tf_op jit(solution)/shard_map/pallas_call | solution.py:223
  21.4 0.0 copy-start
  21.4 1.3 %copy.6 = f32[16,64]{1,0:T(8,128)} copy(f32[16,64]{1,0:T(8,128)} %get-tuple-element.4) | data formatting | bytes 8192
  22.7 0.0 copy-done
  22.7 0.6 %copy.7 = f32[16,16]{1,0:T(8,128)} copy(f32[16,16]{1,0:T(8,128)S(1)} %copy-done) | data formatting | bytes 2048
Async XLA Ops:
  21.4 1.3 %copy-start = (f32[16,16]{1,0:T(8,128)S(1)}, f32[16,16]{1,0:T(8,128)}, u32[]{:S(2)}) copy-start(f32[16,16]{1,0:T(8,128)} %get-tuple-element.5) | copy-start | bytes 3076

commit v2 on v0

v2 whole, which is shorter than its diff:
```python
import functools
import math

import jax
import jax.numpy as jnp
from jax import lax
from jax.experimental import pallas as pl
from jax.experimental.pallas import tpu as pltpu
from jax.sharding import PartitionSpec as P

MESH = pl.DeviceIdType.MESH
LANES = 128
SUBLANES = 8


def split(x):
    high = x.astype(jnp.bfloat16)
    rest = x - high.astype(jnp.float32)
    mid = rest.astype(jnp.bfloat16)
    low = (rest - mid.astype(jnp.float32)).astype(jnp.bfloat16)
    return high, mid, low


def dot(left, right, dims):
    n = left[0].shape[0]

    def one(pieces, weights):
        return lax.dot_general(
            jnp.concatenate(pieces, axis=0),
            weights,
            (dims, ((), ())),
            preferred_element_type=jnp.float32,
        )

    high, mid, low = one(left, right[0]), one(left[:2], right[1]), one(left[:1], right[2])
    small = high[2 * n :] + mid[n:] + low
    return high[:n] + (high[n : 2 * n] + mid[:n] + small)


def remote(src, dst, send, recv, where):
    return pltpu.make_async_remote_copy(
        src_ref=src,
        dst_ref=dst,
        send_sem=send,
        recv_sem=recv,
        device_id=where,
        device_id_type=MESH,
    )


def kernel(
    rows,
    cols,
    panel_hbm,
    kin_hbm,
    out_ref,
    score_ref,
    panel,
    kin,
    kin_high,
    kin_mid,
    kin_low,
    slab,
    block,
    part,
    landed,
    forms,
    panel_sem,
    kin_sem,
    slab_send,
    slab_recv,
    block_send,
    block_recv,
    part_send,
    part_recv,
    forms_send,
    forms_recv,
):
    count = rows * cols
    depth = rows // cols
    plane = depth * cols
    traits, own = panel.shape
    row, col = lax.axis_index("rows"), lax.axis_index("cols")
    me = row * cols + col
    zz = row // depth
    mine = me % plane

    def others(body):
        back = jnp.where(zz < cols // 2, 1, 0)
        base = me + back * count
        sign = 1 - 2 * back

        def step_of(step, carry):
            other = (base + sign * step) % count
            body((other // cols, other % cols), step)
            return carry

        lax.fori_loop(1, count, step_of, 0)

    get_panel = pltpu.make_async_copy(panel_hbm, panel, panel_sem)
    get_panel.start()
    get_kin = pltpu.make_async_copy(kin_hbm, kin, kin_sem)
    get_kin.start()

    barrier = pltpu.get_barrier_semaphore()
    others(
        lambda where, step: pl.semaphore_signal(
            barrier, inc=1, device_id=where, device_id_type=MESH
        )
    )
    get_panel.wait()
    slab[col] = panel[...]
    get_kin.wait()
    kin_high[...], kin_mid[...], kin_low[...] = split(kin[...])
    pl.semaphore_wait(barrier, count - 1)

    keep_block = pltpu.make_async_copy(panel, block.at[mine], block_recv)
    send_block = remote(panel, block.at[mine], block_send, block_recv, (row, zz))
    for step in range(1, rows):
        r = (row + step) % rows
        remote(panel, block.at[mine], block_send, block_recv, (r, zz)).start()

    @pl.when(col == zz)
    def _():
        keep_block.start()

    @pl.when(col != zz)
    def _():
        send_block.start()

    for step in range(1, cols):
        c = (col + step) % cols
        remote(panel, slab.at[col], slab_send, slab_recv, (row, c)).start()

    def wait_bytes(ref, sem):
        pltpu.make_async_copy(ref, ref, sem).wait()

    wait_bytes(slab.at[pl.ds(0, cols - 1)], slab_recv)
    weights = (kin_high[...], kin_mid[...], kin_low[...])
    slab_panel = jnp.concatenate([slab[c] for c in range(cols)], axis=1)
    side = dot(split(slab_panel / math.sqrt(count * own)), weights, ((1,), (0,)))
    wide = tuple(jnp.concatenate([x] * (LANES // traits), axis=0) for x in split(side))

    wait_bytes(block, block_recv)
    block_panel = split(jnp.concatenate([block[m] for m in range(plane)], axis=1))
    spread = dot(block_panel, wide, ((1,), (1,)))
    sublane = lax.broadcasted_iota(jnp.int32, (traits, LANES), 0) % SUBLANES
    group = lax.broadcasted_iota(jnp.int32, (traits, LANES), 1) // traits
    spread = jnp.where(sublane == group, spread, 0.0)
    forms[me] = jnp.sum(spread.reshape(traits // SUBLANES, SUBLANES, LANES), axis=1)
    others(
        lambda where, step: remote(
            forms.at[me], forms.at[me], forms_send, forms_recv, where
        ).start()
    )

    value = dot(block_panel, (kin_high[...], kin_mid[...], kin_low[...]), ((1,), (1,)))
    for c in range(cols):
        part[c] = value[:, c * own : (c + 1) * own]
    for step in range(1, cols):
        c = (col + step) % cols
        remote(part.at[c], landed.at[col], part_send, part_recv, (row, c)).start()
    landed[col] = part[col]

    wait_bytes(landed.at[pl.ds(0, cols - 1)], part_recv)
    result = landed[0]
    for c in range(1, cols):
        result += landed[c]
    out_ref[...] = result

    wait_bytes(block.at[pl.ds(0, rows - 1)], block_send)

    @pl.when(col != zz)
    def _():
        send_block.wait_send()

    wait_bytes(slab.at[pl.ds(0, cols - 1)], slab_send)
    wait_bytes(landed.at[pl.ds(0, cols - 1)], part_send)
    wait_bytes(forms.at[pl.ds(0, count - 1)], forms_send)
    wait_bytes(forms.at[pl.ds(0, count - 1)], forms_recv)
    total = jnp.sum(forms[...], axis=0)
    spread = jnp.concatenate(
        [
            jnp.broadcast_to(total[i : i + 1, :], (SUBLANES, LANES))
            for i in range(traits // SUBLANES)
        ],
        axis=0,
    )
    spread = jnp.where(sublane == group, spread, 0.0)
    score_ref[...] = jnp.sum(spread.T.reshape(LANES // traits, traits, traits), axis=0)


def shards(rows, cols, panel_t, kinship):
    traits, own = panel_t.shape
    plane = rows // cols * cols
    vmem = pltpu.VMEM
    dma = pltpu.SemaphoreType.DMA
    f32, bf16 = jnp.float32, jnp.bfloat16
    chunk = (traits, own)
    return tuple(
        pl.pallas_call(
            functools.partial(kernel, rows, cols),
            out_shape=(vmem(chunk, f32), vmem((traits, traits), f32)),
            in_specs=[pl.BlockSpec(memory_space=pl.ANY)] * 2,
            out_specs=(pl.BlockSpec(memory_space=vmem),) * 2,
            scratch_shapes=[
                vmem(chunk, f32),
                vmem(kinship.shape, f32),
                vmem(kinship.shape, bf16),
                vmem(kinship.shape, bf16),
                vmem(kinship.shape, bf16),
                vmem((cols,) + chunk, f32),
                vmem((plane,) + chunk, f32),
                vmem((cols,) + chunk, f32),
                vmem((cols,) + chunk, f32),
                vmem((rows * cols, traits * traits // LANES, LANES), f32),
            ]
            + [dma(())] * 10,
            compiler_params=pltpu.CompilerParams(collective_id=0, has_side_effects=True),
        )(panel_t, kinship)
    )


def solution(mesh):
    rows, cols = mesh.shape["rows"], mesh.shape["cols"]
    return jax.shard_map(
        functools.partial(shards, rows, cols),
        mesh=mesh,
        in_specs=(P(None, ("rows", "cols")), P("rows", "cols")),
        out_specs=(P(None, ("rows", "cols")), P()),
        check_vma=False,
    )
```

time: 99.9 us -> 18 us (0.18)
  blocking collectives: 81.2 us -> 0 us
  Pallas kernels: 0 us -> 16 us
  between operations: 14.1 us -> 0.64 us
  local copies, waits for them, and re-layouts: 2.39 us -> 1.2 us
    all_gather x1 -> x0, blocking collectives: 44.3 us -> none  [shards(): gathered = lax.all_gather(panel_t, ('rows', 'cols'), axis=1, tiled=True)]
    psum x1 -> x0, blocking collectives: 36.9 us -> none  [shards(): early_sum = lax.psum(contract(slab_panel, partial_value), ('rows', 'cols'))]
    pallas_call x0 -> x1, Pallas kernels: none -> 16 us  [shards(): pl.pallas_call(functools.partial(kernel, rows, cols), out_shape=(vmem(chu...]
    unnamed x5 -> x2, local copies, waits for them, and re-layouts: 2.31 us -> 1.2 us
  transfers between devices with their start and end apart: 1 -> 0, of which waited for: 0 -> 0; matrix products, arithmetic and copies ran while one was open for 1% -> 0% of each run, Pallas kernels for 0% -> 0%
where the time goes in v2:
time: 18 us; the launch traced here: 17.9 us
  Pallas kernels  16 us (89%)
  local copies, waits for them, and re-layouts  1.2 us (7%)
  between operations  0.64 us (4%)
    pallas_call x1, Pallas kernels, shards(): pl.pallas_call(functools.partial(kernel, rows, cols), out_shape=(vmem(chu...  16 us
    unnamed x2, local copies, waits for them, and re-layouts  1.2 us

profile of v2, /device:TPU:0, one launch (start us, length us, event | category | flops | bytes accessed | tf_op | source)
XLA Modules:
  0.0 17.9 jit_solution(1124639132711547569)
XLA Ops:
  0.6 16.0 %shard_map.41 = (f32[16,64]{1,0:T(8,128)S(1)}, f32[16,16]{1,0:T(8,128)S(1)}) custom-call(f32[16,64]{1,0:T(8,128)} %panel_hbm.1, f32[256,512]{1,0:T(8,128)} %kin_hbm.1), custom_call_target="tpu_custom_call" | custom-call | tf_op jit(solution)/shard_map/pallas_call | solution.py:201
  16.7 0.6 %copy.6 = f32[16,64]{1,0:T(8,128)} copy(f32[16,64]{1,0:T(8,128)S(1)} %get-tuple-element.2) | data formatting | bytes 8192
  17.3 0.6 %copy.7 = f32[16,16]{1,0:T(8,128)} copy(f32[16,16]{1,0:T(8,128)S(1)} %get-tuple-element.3) | data formatting | bytes 2048

commit v3 on v2

--- a/solution.py
+++ b/solution.py
@@ -35,6 +35,27 @@
     high, mid, low = one(left, right[0]), one(left[:2], right[1]), one(left[:1], right[2])
     small = high[2 * n :] + mid[n:] + low
     return high[:n] + (high[n : 2 * n] + mid[:n] + small)
+
+
+def fold(x):
+    half = x.shape[0] // 2
+    return jnp.concatenate([x[:half], x[half:]], axis=1)
+
+
+def unfold(x):
+    own = x.shape[1] // 2
+    return jnp.concatenate([x[:, :own], x[:, own:]], axis=0)
+
+
+def join(chunks):
+    own = chunks[0].shape[1] // 2
+    return jnp.concatenate(
+        [
+            jnp.concatenate([x[:, :own] for x in chunks], axis=1),
+            jnp.concatenate([x[:, own:] for x in chunks], axis=1),
+        ],
+        axis=0,
+    )
 
 
 def remote(src, dst, send, recv, where):
@@ -55,6 +76,7 @@
     kin_hbm,
     out_ref,
     score_ref,
+    loaded,
     panel,
     kin,
     kin_high,
@@ -79,39 +101,40 @@
     count = rows * cols
     depth = rows // cols
     plane = depth * cols
-    traits, own = panel.shape
+    traits, own = panel_hbm.shape
     row, col = lax.axis_index("rows"), lax.axis_index("cols")
     me = row * cols + col
     zz = row // depth
     mine = me % plane
 
     def others(body):
-        back = jnp.where(zz < cols // 2, 1, 0)
-        base = me + back * count
-        sign = 1 - 2 * back
-
-        def step_of(step, carry):
-            other = (base + sign * step) % count
-            body((other // cols, other % cols), step)
+        back = zz < cols // 2
+        peers = [(col + step) % cols for step in range(cols)]
+
+        def row_of(step, carry):
+            r = jnp.where(back, row - step, row + step)
+            r = jnp.where(r < 0, r + rows, jnp.where(r >= rows, r - rows, r))
+            for c in peers:
+                body((r, c))
             return carry
 
-        lax.fori_loop(1, count, step_of, 0)
-
-    get_panel = pltpu.make_async_copy(panel_hbm, panel, panel_sem)
+        lax.fori_loop(1, rows, row_of, 0)
+        for c in peers[1:]:
+            body((row, c))
+
+    barrier = pltpu.get_barrier_semaphore()
+    others(
+        lambda where: pl.semaphore_signal(
+            barrier, inc=1, device_id=where, device_id_type=MESH
+        )
+    )
+    get_panel = pltpu.make_async_copy(panel_hbm, loaded, panel_sem)
     get_panel.start()
     get_kin = pltpu.make_async_copy(kin_hbm, kin, kin_sem)
     get_kin.start()
-
-    barrier = pltpu.get_barrier_semaphore()
-    others(
-        lambda where, step: pl.semaphore_signal(
-            barrier, inc=1, device_id=where, device_id_type=MESH
-        )
-    )
     get_panel.wait()
+    panel[...] = fold(loaded[...])
     slab[col] = panel[...]
-    get_kin.wait()
-    kin_high[...], kin_mid[...], kin_low[...] = split(kin[...])
     pl.semaphore_wait(barrier, count - 1)
 
     keep_block = pltpu.make_async_copy(panel, block.at[mine], block_recv)
@@ -135,28 +158,30 @@
     def wait_bytes(ref, sem):
         pltpu.make_async_copy(ref, ref, sem).wait()
 
+    get_kin.wait()
+    kin_high[...], kin_mid[...], kin_low[...] = split(kin[...])
     wait_bytes(slab.at[pl.ds(0, cols - 1)], slab_recv)
     weights = (kin_high[...], kin_mid[...], kin_low[...])
-    slab_panel = jnp.concatenate([slab[c] for c in range(cols)], axis=1)
+    slab_panel = join([slab[c] for c in range(cols)])
     side = dot(split(slab_panel / math.sqrt(count * own)), weights, ((1,), (0,)))
     wide = tuple(jnp.concatenate([x] * (LANES // traits), axis=0) for x in split(side))
 
     wait_bytes(block, block_recv)
-    block_panel = split(jnp.concatenate([block[m] for m in range(plane)], axis=1))
+    block_panel = split(join([block[m] for m in range(plane)]))
     spread = dot(block_panel, wide, ((1,), (1,)))
     sublane = lax.broadcasted_iota(jnp.int32, (traits, LANES), 0) % SUBLANES
     group = lax.broadcasted_iota(jnp.int32, (traits, LANES), 1) // traits
     spread = jnp.where(sublane == group, spread, 0.0)
     forms[me] = jnp.sum(spread.reshape(traits // SUBLANES, SUBLANES, LANES), axis=1)
     others(
-        lambda where, step: remote(
+        lambda where: remote(
             forms.at[me], forms.at[me], forms_send, forms_recv, where
         ).start()
     )
 
     value = dot(block_panel, (kin_high[...], kin_mid[...], kin_low[...]), ((1,), (1,)))
     for c in range(cols):
-        part[c] = value[:, c * own : (c + 1) * own]
+        part[c] = fold(value[:, c * own : (c + 1) * own])
     for step in range(1, cols):
         c = (col + step) % cols
         remote(part.at[c], landed.at[col], part_send, part_recv, (row, c)).start()
@@ -166,7 +191,7 @@
     result = landed[0]
     for c in range(1, cols):
         result += landed[c]
-    out_ref[...] = result
+    out_ref[...] = unfold(result)
 
     wait_bytes(block.at[pl.ds(0, rows - 1)], block_send)
 
@@ -190,20 +215,30 @@
     score_ref[...] = jnp.sum(spread.T.reshape(LANES // traits, traits, traits), axis=0)
 
 
+def finish(value_ref, form_ref, out_ref, score_ref, sems):
+    first = pltpu.make_async_copy(value_ref, out_ref, sems.at[0])
+    second = pltpu.make_async_copy(form_ref, score_ref, sems.at[1])
+    first.start()
+    second.start()
+    first.wait()
+    second.wait()
+
+
 def shards(rows, cols, panel_t, kinship):
     traits, own = panel_t.shape
     plane = rows // cols * cols
     vmem = pltpu.VMEM
     dma = pltpu.SemaphoreType.DMA
     f32, bf16 = jnp.float32, jnp.bfloat16
-    chunk = (traits, own)
-    return tuple(
+    chunk = (traits // 2, 2 * own)
+    value, score = (
         pl.pallas_call(
             functools.partial(kernel, rows, cols),
-            out_shape=(vmem(chunk, f32), vmem((traits, traits), f32)),
+            out_shape=(vmem((traits, own), f32), vmem((traits, traits), f32)),
             in_specs=[pl.BlockSpec(memory_space=pl.ANY)] * 2,
             out_specs=(pl.BlockSpec(memory_space=vmem),) * 2,
             scratch_shapes=[
+                vmem((traits, own), f32),
                 vmem(chunk, f32),
                 vmem(kinship.shape, f32),
                 vmem(kinship.shape, bf16),
@@ -219,6 +254,19 @@
             compiler_params=pltpu.CompilerParams(collective_id=0, has_side_effects=True),
         )(panel_t, kinship)
     )
+    return tuple(
+        pl.pallas_call(
+            finish,
+            out_shape=(
+                jax.ShapeDtypeStruct((traits, own), f32),
+                jax.ShapeDtypeStruct((traits, traits), f32),
+            ),
+            in_specs=[pl.BlockSpec(memory_space=pl.ANY)] * 2,
+            out_specs=(pl.BlockSpec(memory_space=pl.ANY),) * 2,
+            scratch_shapes=[dma((2,))],
+            compiler_params=pltpu.CompilerParams(vmem_limit_bytes=1024 * 1024),
+        )(value, score)
+    )
 
 
 def solution(mesh):

time: 18 us -> 17.1 us (0.950)
  local copies, waits for them, and re-layouts: 1.2 us -> 0 us
  Pallas kernels: 16 us -> 16.3 us
    unnamed x2 -> x0, local copies, waits for them, and re-layouts: 1.2 us -> none
    pallas_call x1 -> x2, Pallas kernels: 16 us -> 16.3 us  [the longest x1 15.7 us: shards(): pl.pallas_call(functools.partial(kernel, rows, cols), out_shape=(vmem((tr...]
where the time goes in v3:
time: 17.1 us; the launch traced here: 16.9 us
  Pallas kernels  16.3 us (95%)
  between operations  0.64 us (4%)
    pallas_call x1, Pallas kernels, shards(): pl.pallas_call(functools.partial(kernel, rows, cols), out_shape=(vmem((tr...  15.7 us
    pallas_call x1, Pallas kernels, shards(): pl.pallas_call(finish, out_shape=(jax.ShapeDtypeStruct((traits, own), f32...  0.62 us

profile of v3, /device:TPU:0, one launch (start us, length us, event | category | flops | bytes accessed | tf_op | source)
XLA Modules:
  0.0 16.9 jit_solution(16675693731016643900)
XLA Ops:
  0.6 15.7 %shard_map.41 = (f32[16,64]{1,0:T(8,128)S(1)}, f32[16,16]{1,0:T(8,128)S(1)}) custom-call(f32[16,64]{1,0:T(8,128)} %panel_hbm.1, f32[256,512]{1,0:T(8,128)} %kin_hbm.1), custom_call_target="tpu_custom_call" | custom-call | tf_op jit(solution)/shard_map/pallas_call | solution.py:235
  16.3 0.6 %shard_map.42 = (f32[16,64]{1,0:T(8,128)}, f32[16,16]{1,0:T(8,128)}) custom-call(f32[16,64]{1,0:T(8,128)S(1)} %get-tuple-element.4.value_ref, f32[16,16]{1,0:T(8,128)S(1)} %get-tuple-element.5.form_ref), custom_call_target="tpu_custom_call" | custom-call | tf_op jit(solution)/shard_map/pallas_call | solution.py:258

commit v4 on v3

--- a/solution.py
+++ b/solution.py
@@ -137,10 +137,15 @@
     slab[col] = panel[...]
     pl.semaphore_wait(barrier, count - 1)
 
+    for step in range(1, cols):
+        c = (col + step) % cols
+        remote(panel, slab.at[col], slab_send, slab_recv, (row, c)).start()
+
     keep_block = pltpu.make_async_copy(panel, block.at[mine], block_recv)
     send_block = remote(panel, block.at[mine], block_send, block_recv, (row, zz))
+    sign = jnp.where(zz < cols // 2, rows - 1, 1)
     for step in range(1, rows):
-        r = (row + step) % rows
+        r = (row + sign * step) % rows
         remote(panel, block.at[mine], block_send, block_recv, (r, zz)).start()
 
     @pl.when(col == zz)
@@ -150,10 +155,6 @@
     @pl.when(col != zz)
     def _():
         send_block.start()
-
-    for step in range(1, cols):
-        c = (col + step) % cols
-        remote(panel, slab.at[col], slab_send, slab_recv, (row, c)).start()
 
     def wait_bytes(ref, sem):
         pltpu.make_async_copy(ref, ref, sem).wait()

time: 17.1 us -> 16.9 us (0.988)
  Pallas kernels: 16.3 us -> 16.1 us
    pallas_call x1, Pallas kernels: 15.7 us -> 15.5 us  [shards(): pl.pallas_call(functools.partial(kernel, rows, cols), out_shape=(vmem((tr...]
where the time goes in v4:
time: 16.9 us; the launch traced here: 16.7 us
  Pallas kernels  16.1 us (95%)
  between operations  0.64 us (4%)
    pallas_call x1, Pallas kernels, shards(): pl.pallas_call(functools.partial(kernel, rows, cols), out_shape=(vmem((tr...  15.5 us
    pallas_call x1, Pallas kernels, shards(): pl.pallas_call(finish, out_shape=(jax.ShapeDtypeStruct((traits, own), f32...  0.62 us

profile of v4, /device:TPU:0, one launch (start us, length us, event | category | flops | bytes accessed | tf_op | source)
XLA Modules:
  0.0 16.7 jit_solution(5127114484347094513)
XLA Ops:
  0.6 15.5 %shard_map.41 = (f32[16,64]{1,0:T(8,128)S(1)}, f32[16,16]{1,0:T(8,128)S(1)}) custom-call(f32[16,64]{1,0:T(8,128)} %panel_hbm.1, f32[256,512]{1,0:T(8,128)} %kin_hbm.1), custom_call_target="tpu_custom_call" | custom-call | tf_op jit(solution)/shard_map/pallas_call | solution.py:236
  16.1 0.6 %shard_map.42 = (f32[16,64]{1,0:T(8,128)}, f32[16,16]{1,0:T(8,128)}) custom-call(f32[16,64]{1,0:T(8,128)S(1)} %get-tuple-element.4.value_ref, f32[16,16]{1,0:T(8,128)S(1)} %get-tuple-element.5.form_ref), custom_call_target="tpu_custom_call" | custom-call | tf_op jit(solution)/shard_map/pallas_call | solution.py:259

commit v5 on v4

--- a/solution.py
+++ b/solution.py
@@ -118,18 +118,18 @@
                 body((r, c))
             return carry
 
-        lax.fori_loop(1, rows, row_of, 0)
+        lax.fori_loop(1, rows, row_of, 0, unroll=True)
         for c in peers[1:]:
             body((row, c))
 
+    get_panel = pltpu.make_async_copy(panel_hbm, loaded, panel_sem)
+    get_panel.start()
     barrier = pltpu.get_barrier_semaphore()
     others(
         lambda where: pl.semaphore_signal(
             barrier, inc=1, device_id=where, device_id_type=MESH
         )
     )
-    get_panel = pltpu.make_async_copy(panel_hbm, loaded, panel_sem)
-    get_panel.start()
     get_kin = pltpu.make_async_copy(kin_hbm, kin, kin_sem)
     get_kin.start()
     get_panel.wait()

time: 16.9 us -> 16.9 us (level)
  no operation moved by 1% of the time
where the time goes in v5:
time: 16.9 us; the launch traced here: 16.7 us
  Pallas kernels  16.1 us (95%)
  between operations  0.64 us (4%)
    pallas_call x1, Pallas kernels, shards(): pl.pallas_call(functools.partial(kernel, rows, cols), out_shape=(vmem((tr...  15.5 us
    pallas_call x1, Pallas kernels, shards(): pl.pallas_call(finish, out_shape=(jax.ShapeDtypeStruct((traits, own), f32...  0.62 us

profile of v5, /device:TPU:0, one launch (start us, length us, event | category | flops | bytes accessed | tf_op | source)
XLA Modules:
  0.0 16.7 jit_solution(9055593227557559496)
XLA Ops:
  0.6 15.5 %shard_map.41 = (f32[16,64]{1,0:T(8,128)S(1)}, f32[16,16]{1,0:T(8,128)S(1)}) custom-call(f32[16,64]{1,0:T(8,128)} %panel_hbm.1, f32[256,512]{1,0:T(8,128)} %kin_hbm.1), custom_call_target="tpu_custom_call" | custom-call | tf_op jit(solution)/shard_map/pallas_call | solution.py:236
  16.1 0.6 %shard_map.42 = (f32[16,64]{1,0:T(8,128)}, f32[16,16]{1,0:T(8,128)}) custom-call(f32[16,64]{1,0:T(8,128)S(1)} %get-tuple-element.4.value_ref, f32[16,16]{1,0:T(8,128)S(1)} %get-tuple-element.5.form_ref), custom_call_target="tpu_custom_call" | custom-call | tf_op jit(solution)/shard_map/pallas_call | solution.py:259
